TPU v7x, 256 devices: a whole 4x4x8 slice. The times are simulated.
256 devices in a mesh: sub: 32 (over x, z_hi, core), coarse: 8 (over z_lo, y).
Axes of the slice: x: 4, y: 4, z: 8 (z_hi: 4, z_lo: 2; z = z_hi * 2 + z_lo), core: 2. Of those that a mesh axis runs over, the one named last changes fastest.
Arguments:
- residual_parts: bfloat16 [32, 8, 4, 256, 512], P('sub', 'coarse'), may hold values from -6 to 6
- face_slot: int32 [32, 8, 4], P('sub', 'coarse'), may hold values from 0 to 3, each once within a row
- face_order: int32 [32, 8, 4, 512], P('sub', 'coarse'), may hold values from 0 to 511, each once within a row
- face_scale: float32 [32, 8, 4], P('sub', 'coarse'), may hold values from 0 to 1, as said below
- vertex_unknowns: int32 [32, 8, 256], P('sub', 'coarse'), may hold values from 0 to 2047, all different within a row
- front_inverse: bfloat16 [32, 8, 2048, 2048], P('sub', 'coarse')
- coarse_basis: bfloat16 [32, 8, 2048, 256], P('sub', 'coarse'), may hold values from -0.125 to 0.125
- coarse_inverse: bfloat16 [32, 2048, 2048], P('sub', None, 'coarse'), as said below
- thermal_handoff: bfloat16 [32, 2048, 128], P('sub'), may hold values from -0.125 to 0.125
- chain_transfer: float32 [32, 128, 128], P('sub')
- coupling_in: bfloat16 [32, 128, 2048], P('sub', None, 'coarse'), may hold values from -0.5 to 0.5
Outputs:
- correction: bfloat16 [32, 8, 4, 256, 512], P('sub', 'coarse')
Inputs may be any that keep to these rules, and one draw needn't show every extreme that they name: `face_slot`: each row is a permutation of 0 to 3. `face_order`: each row is a permutation of 0 to 511. `vertex_unknowns`: the 256 entries of each subdomain are distinct. `face_scale`: the two weights of a shared face sum to one; a face on the outer boundary has weight one. `coarse_inverse`: each line's matrix is symmetric.
All inputs are finite; a program needn't handle non-finite values.
Results may differ from a plain program's by a relative error of at most 0.0059.
Values may be sent and summed in bfloat16 or wider, within the bound.
No kernel may reach another device: no remote copies, remote signals or barrier semaphores. Data moves between devices by JAX's collectives and lax.ppermute only.
A program may use at most 128 MiB of HBM per device.

v0:
```python
import jax
import jax.numpy as jnp
from jax import lax
from jax.sharding import PartitionSpec as P

HIGHEST = lax.Precision.HIGHEST


def with_halo(block, sides, width):
    for axis, dim in sides:
        count = lax.axis_size(axis)
        forward = [(i, i + 1) for i in range(count - 1)]
        backward = [(target, source) for source, target in forward]
        low = lax.ppermute(
            lax.slice_in_dim(block, block.shape[dim] - width, None, axis=dim), axis, forward
        )
        high = lax.ppermute(lax.slice_in_dim(block, 0, width, axis=dim), axis, backward)
        block = jnp.concatenate([low, block, high], axis=dim)
    return block


def carried_in(array, axis, combine, identity):
    peers, mine = (lax.axis_size(axis), lax.axis_index(axis))
    everything = jax.tree.map(lambda part: lax.all_gather(part, axis), array)
    start = jax.tree.map(
        lambda part, zero: jnp.broadcast_to(jnp.asarray(zero, part.dtype), part.shape),
        array,
        identity,
    )

    def step(k, before):
        reached = k < mine
        new = combine(before, jax.tree.map(lambda part: part[k], everything))
        return jax.tree.map(lambda a, b: jnp.where(reached, a, b), new, before)

    return lax.fori_loop(0, peers, step, start)


def build_tables(face_slot, face_order, table_type):
    face_count, block_size = face_order.shape
    slot_table = (
        face_slot[:, None] == lax.broadcasted_iota(jnp.int32, (face_count, face_count), 1)
    ).astype(table_type)
    order_table = (
        face_order[:, :, None]
        == lax.broadcasted_iota(jnp.int32, (face_count, block_size, block_size), 2)
    ).astype(table_type)
    return (slot_table, order_table)


def to_canonical(values, tables):
    slot_table, order_table = tables
    ordered = jnp.einsum(
        "snk,sjk->snj", values, order_table, preferred_element_type=jnp.float32, precision=HIGHEST
    ).astype(values.dtype)
    return jnp.einsum(
        "ds,snj->dnj", slot_table, ordered, preferred_element_type=jnp.float32, precision=HIGHEST
    ).astype(values.dtype)


def from_canonical(values, tables):
    slot_table, order_table = tables
    by_face = jnp.einsum(
        "ds,dnj->snj", slot_table, values, preferred_element_type=jnp.float32, precision=HIGHEST
    ).astype(values.dtype)
    return jnp.einsum(
        "snj,sjk->snk", by_face, order_table, preferred_element_type=jnp.float32, precision=HIGHEST
    ).astype(values.dtype)


def trade_faces(face_values):
    along_sub = with_halo(face_values[0:2], (("sub", 0),), 1)
    along_coarse = with_halo(face_values[2:4], (("coarse", 0),), 1)
    return jnp.stack([along_sub[0], along_sub[3], along_coarse[0], along_coarse[3]], 0)


def per_device(
    residual_parts,
    face_slot,
    face_order,
    face_scale,
    vertex_unknowns,
    front_inverse,
    coarse_basis,
    coarse_inverse,
    thermal_handoff,
    chain_transfer,
    coupling_in,
):
    own_parts = residual_parts[0, 0]
    own_slot = face_slot[0, 0]
    own_order = face_order[0, 0]
    own_scale = face_scale[0, 0][:, None, None]
    face_count, sample_count, block_size = own_parts.shape
    reduced_precision_tables = build_tables(own_slot, own_order, jnp.bfloat16)
    canon = to_canonical(own_parts, reduced_precision_tables)
    beside = trade_faces(canon)
    averaged = (own_scale * (canon.astype(jnp.float32) + beside.astype(jnp.float32))).astype(
        jnp.bfloat16
    )
    local_residual = from_canonical(averaged, reduced_precision_tables)
    own_primal = vertex_unknowns[0, 0]
    positions = lax.broadcasted_iota(jnp.int32, (own_primal.shape[0], face_count * block_size), 1)
    hits = jnp.sum((own_primal[:, None] == positions).astype(jnp.int32), axis=0)
    dual_mask = (1 - hits).astype(jnp.bfloat16).reshape(face_count, 1, block_size)
    inverse_blocks = front_inverse[0, 0].reshape(face_count, block_size, face_count, block_size)
    dual_part = (
        jnp.einsum(
            "gnj,gjfk->fnk",
            local_residual * dual_mask,
            inverse_blocks,
            preferred_element_type=jnp.float32,
        )
        * dual_mask
    )
    basis_blocks = coarse_basis[0, 0].reshape(face_count, block_size, -1)
    coarse_residual = jnp.einsum(
        "gnj,gjc->nc", local_residual, basis_blocks, preferred_element_type=jnp.float32
    ).astype(jnp.bfloat16)
    primal_count = coarse_residual.shape[1]
    line_block = coarse_inverse[0]
    line_outflow = thermal_handoff[0]
    channel_count = line_outflow.shape[1]
    line_base = lax.dot_general(
        line_block,
        lax.all_gather(coarse_residual, "coarse", axis=1, tiled=True),
        (((0,), (1,)), ((), ())),
        preferred_element_type=jnp.float32,
    )
    own_rows = lax.dynamic_slice_in_dim(
        line_outflow, lax.axis_index("coarse") * primal_count, primal_count, 0
    )
    inflow = lax.psum(
        jnp.dot(coarse_residual, own_rows, preferred_element_type=jnp.float32), "coarse"
    )
    transfer = chain_transfer[0]

    def compose(earlier, later):
        joined_map = jnp.dot(earlier[0], later[0], precision=HIGHEST)
        joined_state = jnp.dot(earlier[1], later[0], precision=HIGHEST) + later[1]
        return (joined_map, joined_state)

    identity = (jnp.eye(channel_count, dtype=jnp.float32), jnp.zeros_like(inflow))
    upstream_map, carried = carried_in((transfer, inflow), "sub", compose, identity)
    carried_term = lax.dot_general(
        coupling_in[0].astype(jnp.float32), carried, (((0,), (1,)), ((), ())), precision=HIGHEST
    )
    global_coarse_answer = (line_base + carried_term).astype(jnp.bfloat16)
    subregion_iterate = dual_part + jnp.einsum(
        "cn,gjc->gnj", global_coarse_answer, basis_blocks, preferred_element_type=jnp.float32
    )
    exact_tables = build_tables(own_slot, own_order, jnp.float32)
    weighted = (own_scale * to_canonical(subregion_iterate, exact_tables)).astype(jnp.bfloat16)
    beside_again = trade_faces(weighted)
    summed = (weighted.astype(jnp.float32) + beside_again.astype(jnp.float32)).astype(jnp.bfloat16)
    return from_canonical(summed, reduced_precision_tables)[None, None]


def solution(mesh):
    placed = (
        P("sub", "coarse", None, None, None),
        P("sub", "coarse", None),
        P("sub", "coarse", None, None),
        P("sub", "coarse", None),
        P("sub", "coarse", None),
        P("sub", "coarse", None, None),
        P("sub", "coarse", None, None),
        P("sub", None, "coarse"),
        P("sub", None, None),
        P("sub", None, None),
        P("sub", None, "coarse"),
    )
    return jax.shard_map(
        per_device,
        mesh=mesh,
        in_specs=placed,
        out_specs=P("sub", "coarse", None, None, None),
        check_vma=False,
    )
```

profile of v0, /device:TPU:26, one launch (start us, length us, event | category | flops | bytes accessed | tf_op | source)
XLA Modules:
  0.0 419.8 jit_solution(5209459540740825076)
XLA Ops:
  6.5 2.4 fusion.30
  11.1 2.3 fusion.70
  13.4 1.9 collective-permute-start
  15.4 7.6 %collective-permute-start.1 = (bf16[1,256,512]{2,0,1:T(2,128)(2,1)}, bf16[1,256,512]{2,0,1:T(2,128)(2,1)}, u32[]{:S(2)}, u32[]{:S(2)}) collective-permute-start(bf16[1,256,512]{2,0,1:T(2,128)(2,1)} %get-tuple-element.150), channel_id=1, source_target_pairs={{8,0},{16,8},{24,16},{32,24},{40,32},{48,40},{56,48},{64,56},{72,6... | collective-permute-start | bytes 786440 | tf_op jit(solution)/shard_map/ppermute | solution.py:17
  23.0 2.6 collective-permute-start.2
  25.6 3.3 collective-permute-start.3
  28.8 5.6 %collective-permute-done = bf16[1,256,512]{2,0,1:T(2,128)(2,1)} collective-permute-done((bf16[1,256,512]{2,0,1:T(2,128)(2,1)}, bf16[1,256,512]{2,0,1:T(2,128)(2,1)}, u32[]{:S(2)}, u32[]{:S(2)}) %collective-permute-start) | collective-permute-done | bytes 262176 | tf_op jit(solution)/shard_map/ppermute | solution.py:14
  35.6 6.2 %collective-permute-done.2 = bf16[1,256,512]{2,0,1:T(2,128)(2,1)} collective-permute-done((bf16[1,256,512]{2,0,1:T(2,128)(2,1)S(1)}, bf16[1,256,512]{2,0,1:T(2,128)(2,1)}, u32[]{:S(2)}, u32[]{:S(2)}) %collective-permute-start.2) | collective-permute-done | bytes 262176 | tf_op jit(solution)/shard_map/ppermute | solution.py:14
  41.8 5.4 %collective-permute-done.3 = bf16[1,256,512]{2,0,1:T(2,128)(2,1)} collective-permute-done((bf16[1,256,512]{2,0,1:T(2,128)(2,1)S(1)}, bf16[1,256,512]{2,0,1:T(2,128)(2,1)}, u32[]{:S(2)}, u32[]{:S(2)}) %collective-permute-start.3) | collective-permute-done | bytes 262176 | tf_op jit(solution)/shard_map/ppermute | solution.py:17
  47.2 4.5 %convolution_convert_fusion.1 = bf16[4,256,512]{2,0,1:T(4,128)(2,1)S(1)} fusion(bf16[4,256,512]{2,0,1:T(4,128)(2,1)S(1)} %convolution_convert_fusion.2, bf16[1,256,512]{2,0,1:T(2,128)(2,1)} %collective-permute-done.3, bf16[1,256,512]{2,0,1:T(2,128)(2,1)} %collective-permute-done.2, bf16[1,256,512]{2,0,1:T(2,128)(2,1)} %collective-permute-done.1, ...), kind=kOutput, calls=%fused_computation.36 | convolution fusion | flops 11010064 | bytes 3145760 | tf_op jit(solution)/shard_map/ds,dnj->snj/dot_general | solution.py:63
  51.7 1.4 fusion.27
  54.5 1.7 convolution_bitcast_fusion.2
  57.9 75.5 %all-reduce.2.cloned.1.call-done = f32[1,256,128]{2,1,0:T(8,128)} async-done(((f32[1,256,128]{2,1,0:T(8,128)}), f32[1,256,128]{2,1,0:T(8,128)}) %all-reduce.2.cloned.1.call-update) | async-done | bytes 131088 | tf_op jit(solution)/shard_map/psum | solution.py:133
  133.9 14.5 %reshape_squeeze.6 = bf16[4,512,4,512]{3,2,1,0:T(4,128)(2,1)} reshape(bf16[1,1,2048,2048]{3,2,1,0:T(8,128)(2,1)} %param.18) | data formatting | bytes 16777216 | tf_op jit(solution)/shard_map/reshape;squeeze | solution.py:106
  148.4 6.5 %fusion.9 = f32[256,4,512,1]{2,0,3,1:T(8,128)S(1)} fusion(bf16[4,512,4,512]{3,2,1,0:T(4,128)(2,1)} %reshape_squeeze.6, bf16[4,256,512]{2,1,0:T(8,128)(2,1)} %copy-done.2, bf16[4,512]{1,0:T(4,128)(2,1)S(1)} %convert_element_type.89), kind=kOutput, calls=%fused_computation.11 | convolution fusion | flops 2149580800 | bytes 11538432 | tf_op jit(solution)/shard_map/gnj,gjfk->fnk/dot_general | solution.py:108
  155.0 22.1 %all-gather.4.cloned.1.call-done = bf16[256,2048]{1,0:T(8,128)(2,1)} async-done(((bf16[256,256]{1,0:T(8,128)(2,1)}), bf16[256,2048]{1,0:T(8,128)(2,1)}) %all-gather.4.cloned.1.call-update) | async-done | bytes 1048592 | tf_op jit(solution)/shard_map/all_gather | solution.py:126
  177.1 2.7 fusion.48
  179.8 54.5 %all-gather.6.cloned.1.call-done = f32[32,128,128]{2,1,0:T(8,128)} async-done(((f32[1,128,128]{2,1,0:T(8,128)}), f32[32,128,128]{2,1,0:T(8,128)}) %all-gather.6.cloned.1.call-update) | async-done | bytes 2097168 | tf_op jit(solution)/shard_map/all_gather | solution.py:24
  234.3 61.3 %all-gather.8.cloned.1.call-done = f32[32,256,128]{2,1,0:T(8,128)} async-done(((f32[1,256,128]{2,1,0:T(8,128)}), f32[32,256,128]{2,1,0:T(8,128)}) %all-gather.8.cloned.1.call-update) | async-done | bytes 4194320 | tf_op jit(solution)/shard_map/all_gather | solution.py:24
  295.6 71.3 %while.14 = (s32[]{:T(128)}, f32[256,128]{0,1:T(8,128)S(1)}, s32[]{:T(128)}, f32[32,128,128]{2,1,0:T(8,128)}, f32[32,256,128]{2,1,0:T(8,128)}, /*index=5*/s32[]{:T(128)}, s32[]{:T(128)}) while((s32[]{:T(128)}, f32[256,128]{0,1:T(8,128)S(1)}, s32[]{:T(128)}, f32[32,128,128]{2,1,0:T(8,128)}, f32[32,256,128]{2,1,0:T(8,128)}, ...), condition=%wide.region_3.4_spmd.clone, body=%wide.region_2.3_spmd.clone.sunk | while | flops 50462724 | bytes 1378403 | solution.py:36
  368.7 2.8 fusion.12
  371.5 3.3 multiply_convert_fusion
  374.8 1.6 fusion.69
  376.4 2.2 collective-permute-start.4
  378.6 6.4 %collective-permute-start.5 = (bf16[1,256,512]{2,0,1:T(2,128)(2,1)S(1)}, bf16[1,256,512]{2,0,1:T(2,128)(2,1)S(1)}, u32[]{:S(2)}, u32[]{:S(2)}) collective-permute-start(bf16[1,256,512]{2,0,1:T(2,128)(2,1)S(1)} %get-tuple-element.146), channel_id=1, source_target_pairs={{8,0},{16,8},{24,16},{32,24},{40,32},{48,40},{56,48},{64,56},{72,6... | collective-permute-start | bytes 786440 | tf_op jit(solution)/shard_map/ppermute | solution.py:17
  385.0 2.1 collective-permute-start.6
  387.1 3.7 collective-permute-start.7
  390.9 5.8 %collective-permute-done.4 = bf16[1,256,512]{2,0,1:T(2,128)(2,1)S(1)} collective-permute-done((bf16[1,256,512]{2,0,1:T(2,128)(2,1)S(1)}, bf16[1,256,512]{2,0,1:T(2,128)(2,1)S(1)}, u32[]{:S(2)}, u32[]{:S(2)}) %collective-permute-start.4) | collective-permute-done | bytes 262176 | tf_op jit(solution)/shard_map/ppermute | solution.py:14
  397.1 5.4 %collective-permute-done.6 = bf16[1,256,512]{2,0,1:T(2,128)(2,1)S(1)} collective-permute-done((bf16[1,256,512]{2,0,1:T(2,128)(2,1)S(1)}, bf16[1,256,512]{2,0,1:T(2,128)(2,1)S(1)}, u32[]{:S(2)}, u32[]{:S(2)}) %collective-permute-start.6) | collective-permute-done | bytes 262176 | tf_op jit(solution)/shard_map/ppermute | solution.py:14
  402.4 5.8 %collective-permute-done.7 = bf16[1,256,512]{2,0,1:T(2,128)(2,1)S(1)} collective-permute-done((bf16[1,256,512]{2,0,1:T(2,128)(2,1)S(1)}, bf16[1,256,512]{2,0,1:T(2,128)(2,1)S(1)}, u32[]{:S(2)}, u32[]{:S(2)}) %collective-permute-start.7) | collective-permute-done | bytes 262176 | tf_op jit(solution)/shard_map/ppermute | solution.py:17
  408.2 2.9 convolution_convert_fusion
  411.1 2.2 fusion.29
  (166 shorter events, 78.6 us)
Async XLA Ops:
  6.5 46.5 %copy-start = (bf16[1,1,2048,256]{3,2,1,0:T(8,128)(2,1)S(1)}, bf16[1,1,2048,256]{3,2,1,0:T(8,128)(2,1)}, u32[]{:S(2)}) copy-start(bf16[1,1,2048,256]{3,2,1,0:T(8,128)(2,1)} %param.19) | copy-start | bytes 3145732
  6.5 126.9 %all-reduce.2.cloned.1.call-start = ((), (), s32[]{:S(2)}) async-start(), calls=%async_computation.2 | async-start | bytes 262144 | tf_op jit(solution)/shard_map/psum | solution.py:133
  6.5 3.5 copy-start.4
  11.1 36.1 %copy-start.7 = (f32[1,1,4]{2,1,0:T(1,128)S(1)}, f32[1,1,4]{2,1,0:T(1,128)}, u32[]{:S(2)}) copy-start(f32[1,1,4]{2,1,0:T(1,128)} %param.16) | copy-start | bytes 52
  13.4 21.0 %collective-permute-start = (bf16[1,256,512]{2,0,1:T(2,128)(2,1)}, bf16[1,256,512]{2,0,1:T(2,128)(2,1)}, u32[]{:S(2)}, u32[]{:S(2)}) collective-permute-start(bf16[1,256,512]{2,0,1:T(2,128)(2,1)} %get-tuple-element.147), channel_id=1, source_target_pairs={{0,8},{8,16},{16,24},{24,32},{32,40},{40,48},{48,56},{56,64},{64,7... | collective-permute-start | bytes 786440 | tf_op jit(solution)/shard_map/ppermute | solution.py:14
  15.4 20.3 %collective-permute-start.1 = (bf16[1,256,512]{2,0,1:T(2,128)(2,1)}, bf16[1,256,512]{2,0,1:T(2,128)(2,1)}, u32[]{:S(2)}, u32[]{:S(2)}) collective-permute-start(bf16[1,256,512]{2,0,1:T(2,128)(2,1)} %get-tuple-element.150), channel_id=1, source_target_pairs={{8,0},{16,8},{24,16},{32,24},{40,32},{48,40},{56,48},{64,56},{72,6... | collective-permute-start | bytes 786440 | tf_op jit(solution)/shard_map/ppermute | solution.py:17
  23.0 18.8 %collective-permute-start.2 = (bf16[1,256,512]{2,0,1:T(2,128)(2,1)S(1)}, bf16[1,256,512]{2,0,1:T(2,128)(2,1)}, u32[]{:S(2)}, u32[]{:S(2)}) collective-permute-start(bf16[1,256,512]{2,0,1:T(2,128)(2,1)S(1)} %get-tuple-element.149), channel_id=1, source_target_pairs={{0,1},{1,2},{2,3},{3,4},{4,5},{5,6},{6,7},{8,9},{9,10},{10,11},{11... | collective-permute-start | bytes 786440 | tf_op jit(solution)/shard_map/ppermute | solution.py:14
  25.6 21.6 %collective-permute-start.3 = (bf16[1,256,512]{2,0,1:T(2,128)(2,1)S(1)}, bf16[1,256,512]{2,0,1:T(2,128)(2,1)}, u32[]{:S(2)}, u32[]{:S(2)}) collective-permute-start(bf16[1,256,512]{2,0,1:T(2,128)(2,1)S(1)} %get-tuple-element.148), channel_id=1, source_target_pairs={{1,0},{2,1},{3,2},{4,3},{5,4},{6,5},{7,6},{9,8},{10,9},{11,10},{12... | collective-permute-start | bytes 786440 | tf_op jit(solution)/shard_map/ppermute | solution.py:17
  47.2 4.5 %copy-start.3 = (s32[1,1,4,512]{3,2,1,0:T(4,128)S(1)}, s32[1,1,4,512]{3,2,1,0:T(4,128)}, u32[]{:S(2)}) copy-start(s32[1,1,4,512]{3,2,1,0:T(4,128)} %param.15) | copy-start | bytes 24580
  53.1 1.0 copy-start.2
  53.1 80.5 %copy-start.6 = (s32[1,1,256]{2,1,0:T(1,128)S(1)}, s32[1,1,256]{2,1,0:T(1,128)}, u32[]{:S(2)}) copy-start(s32[1,1,256]{2,1,0:T(1,128)} %param.17) | copy-start | bytes 3076
  54.5 1.8 copy-start.1
  56.2 120.8 %all-gather.4.cloned.1.call-start = ((), (), s32[]{:S(2)}) async-start(), calls=%async_computation | async-start | bytes 1179648 | tf_op jit(solution)/shard_map/all_gather | solution.py:126
  57.0 177.3 %all-gather.6.cloned.1.call-start = ((), (), s32[]{:S(2)}) async-start(), calls=%async_computation.1 | async-start | bytes 2162688 | tf_op jit(solution)/shard_map/all_gather | solution.py:24
  57.7 237.9 %all-gather.8.cloned.1.call-start = ((), (), s32[]{:S(2)}) async-start(), calls=%async_computation.3 | async-start | bytes 4325376 | tf_op jit(solution)/shard_map/all_gather | solution.py:24
  368.7 2.8 copy-start.5
  368.7 2.8 copy-start.8
  376.4 20.3 %collective-permute-start.4 = (bf16[1,256,512]{2,0,1:T(2,128)(2,1)S(1)}, bf16[1,256,512]{2,0,1:T(2,128)(2,1)S(1)}, u32[]{:S(2)}, u32[]{:S(2)}) collective-permute-start(bf16[1,256,512]{2,0,1:T(2,128)(2,1)S(1)} %get-tuple-element.143), channel_id=1, source_target_pairs={{0,8},{8,16},{16,24},{24,32},{32,40},{40,48},{48,56},{56,64},{64,7... | collective-permute-start | bytes 786440 | tf_op jit(solution)/shard_map/ppermute | solution.py:14
  378.6 18.5 %collective-permute-start.5 = (bf16[1,256,512]{2,0,1:T(2,128)(2,1)S(1)}, bf16[1,256,512]{2,0,1:T(2,128)(2,1)S(1)}, u32[]{:S(2)}, u32[]{:S(2)}) collective-permute-start(bf16[1,256,512]{2,0,1:T(2,128)(2,1)S(1)} %get-tuple-element.146), channel_id=1, source_target_pairs={{8,0},{16,8},{24,16},{32,24},{40,32},{48,40},{56,48},{64,56},{72,6... | collective-permute-start | bytes 786440 | tf_op jit(solution)/shard_map/ppermute | solution.py:17
  385.0 17.5 %collective-permute-start.6 = (bf16[1,256,512]{2,0,1:T(2,128)(2,1)S(1)}, bf16[1,256,512]{2,0,1:T(2,128)(2,1)S(1)}, u32[]{:S(2)}, u32[]{:S(2)}) collective-permute-start(bf16[1,256,512]{2,0,1:T(2,128)(2,1)S(1)} %get-tuple-element.145), channel_id=1, source_target_pairs={{0,1},{1,2},{2,3},{3,4},{4,5},{5,6},{6,7},{8,9},{9,10},{10,11},{11... | collective-permute-start | bytes 786440 | tf_op jit(solution)/shard_map/ppermute | solution.py:14
  387.1 21.1 %collective-permute-start.7 = (bf16[1,256,512]{2,0,1:T(2,128)(2,1)S(1)}, bf16[1,256,512]{2,0,1:T(2,128)(2,1)S(1)}, u32[]{:S(2)}, u32[]{:S(2)}) collective-permute-start(bf16[1,256,512]{2,0,1:T(2,128)(2,1)S(1)} %get-tuple-element.144), channel_id=1, source_target_pairs={{1,0},{2,1},{3,2},{4,3},{5,4},{6,5},{7,6},{9,8},{10,9},{11,10},{12... | collective-permute-start | bytes 786440 | tf_op jit(solution)/shard_map/ppermute | solution.py:17
Sparse Core Ops, SparseCore 0:
  56.3 77.0 all-reduce.1
  135.3 41.7 all-gather.3
  180.0 54.2 all-gather.5
  237.0 58.5 all-gather.7
where the time goes:
time: 423 us; the launch traced here: 420 us
  waiting for transfers between devices  251 us (59%)
  matrix products  70.6 us (17%)
  local copies, waits for them, and re-layouts  53.2 us (13%)
  starting transfers between devices  30.1 us (7%)
  between operations  13.4 us (3%)
    all_gather x2, waiting for transfers between devices, carried_in(): everything = jax.tree.map(lambda part: lax.all_gather(part, axis), array)  116 us
    psum x1, waiting for transfers between devices, per_device(): lax.psum(jnp.dot(coarse_residual, own_rows, preferred_element_type=jnp.fl...  75.5 us
    dot_general x32, matrix products, compose(): joined_state = jnp.dot(earlier[1], later[0], precision=HIGHEST) + later[1]  37 us
    dynamic_slice x64, local copies, waits for them, and re-layouts, step(): new = combine(before, jax.tree.map(lambda part: part[k], everything))  32.4 us
    ppermute x4, waiting for transfers between devices, with_halo(): lax.ppermute(lax.slice_in_dim(block, block.shape[dim] - width, None, axis...  23 us
    all_gather x1, waiting for transfers between devices, per_device(): lax.all_gather(coarse_residual, 'coarse', axis=1, tiled=True)  22.1 us
    ppermute x4, starting transfers between devices, with_halo(): lax.ppermute(lax.slice_in_dim(block, 0, width, axis=dim), axis, backward)  21 us
    another operation x1, local copies, waits for them, and re-layouts, per_device(): front_inverse[0, 0].reshape(face_count, block_size, face_count, block_size)  14.5 us
  transfers between devices with their start and end apart: 12, of which 12 were waited for; matrix products, arithmetic and copies ran while one was open for 6% of the time, Pallas kernels for 0%

commit v1 on v0

--- a/solution.py
+++ b/solution.py
@@ -4,6 +4,11 @@
 from jax.sharding import PartitionSpec as P
 
 HIGHEST = lax.Precision.HIGHEST
+
+
+def fix_routes_all(mine_x):
+    w2 = jnp.stack([mine_x for _ in range(lax.axis_size("coarse"))], 0)
+    return jnp.concatenate(lax.all_to_all(w2, "coarse", split_axis=0, concat_axis=0), 1)
 
 
 def with_halo(block, sides, width):
@@ -123,7 +128,7 @@
     channel_count = line_outflow.shape[1]
     line_base = lax.dot_general(
         line_block,
-        lax.all_gather(coarse_residual, "coarse", axis=1, tiled=True),
+        fix_routes_all(coarse_residual),
         (((0,), (1,)), ((), ())),
         preferred_element_type=jnp.float32,
     )

time: 423 us -> 325 us (0.77)
  waiting for transfers between devices: 251 us -> 145 us
  starting transfers between devices: 30.1 us -> 36.1 us
    all_gather x2, waiting for transfers between devices: 116 us -> 31.2 us  [carried_in(): everything = jax.tree.map(lambda part: lax.all_gather(part, axis), array)]
    all_gather x1 -> x0, waiting for transfers between devices: 22.1 us -> none  [per_device(): lax.all_gather(coarse_residual, 'coarse', axis=1, tiled=True)]
    all_to_all x0 -> x1, starting transfers between devices: none -> 6.2 us  [fix_routes_all(): lax.all_to_all(w2, 'coarse', split_axis=0, concat_axis=0)]
  transfers between devices with their start and end apart: 12 -> 12, of which waited for: 12 -> 9; matrix products, arithmetic and copies ran while one was open for 6% -> 8% of each run, Pallas kernels for 0% -> 0%
where the time goes in v1:
time: 325 us; the launch traced here: 323 us
  waiting for transfers between devices  145 us (45%)
  matrix products  68.8 us (21%)
  local copies, waits for them, and re-layouts  55.2 us (17%)
  starting transfers between devices  36.1 us (11%)
  between operations  15.1 us (5%)
    psum x1, waiting for transfers between devices, per_device(): lax.psum(jnp.dot(coarse_residual, own_rows, preferred_element_type=jnp.fl...  76.7 us
    dot_general x32, matrix products, compose(): joined_state = jnp.dot(earlier[1], later[0], precision=HIGHEST) + later[1]  37 us
    dynamic_slice x64, local copies, waits for them, and re-layouts, step(): new = combine(before, jax.tree.map(lambda part: part[k], everything))  32.4 us
    all_gather x2, waiting for transfers between devices, carried_in(): everything = jax.tree.map(lambda part: lax.all_gather(part, axis), array)  31.2 us
    ppermute x4, waiting for transfers between devices, with_halo(): lax.ppermute(lax.slice_in_dim(block, block.shape[dim] - width, None, axis...  23.1 us
    ppermute x4, starting transfers between devices, with_halo(): lax.ppermute(lax.slice_in_dim(block, 0, width, axis=dim), axis, backward)  20.5 us
    another operation x1, local copies, waits for them, and re-layouts, per_device(): front_inverse[0, 0].reshape(face_count, block_size, face_count, block_size)  14.6 us
    ppermute x4, waiting for transfers between devices, with_halo(): lax.ppermute(lax.slice_in_dim(block, 0, width, axis=dim), axis, backward)  14 us
  transfers between devices with their start and end apart: 12, of which 9 were waited for; matrix products, arithmetic and copies ran while one was open for 8% of the time, Pallas kernels for 0%

profile of v1, /device:TPU:26, one launch (start us, length us, event | category | flops | bytes accessed | tf_op | source)
XLA Modules:
  0.0 322.6 jit_solution(11677442273700182877)
XLA Ops:
  7.4 2.4 fusion.30
  11.9 2.3 fusion.70
  14.3 1.9 collective-permute-start
  16.2 7.6 %collective-permute-start.1 = (bf16[1,256,512]{2,0,1:T(2,128)(2,1)}, bf16[1,256,512]{2,0,1:T(2,128)(2,1)}, u32[]{:S(2)}, u32[]{:S(2)}) collective-permute-start(bf16[1,256,512]{2,0,1:T(2,128)(2,1)} %get-tuple-element.155), channel_id=1, source_target_pairs={{8,0},{16,8},{24,16},{32,24},{40,32},{48,40},{56,48},{64,56},{72,6... | collective-permute-start | bytes 786440 | tf_op jit(solution)/shard_map/ppermute | solution.py:22
  23.8 2.6 collective-permute-start.2
  26.4 3.3 %collective-permute-start.3 = (bf16[1,256,512]{2,0,1:T(2,128)(2,1)S(1)}, bf16[1,256,512]{2,0,1:T(2,128)(2,1)}, u32[]{:S(2)}, u32[]{:S(2)}) collective-permute-start(bf16[1,256,512]{2,0,1:T(2,128)(2,1)S(1)} %get-tuple-element.153), channel_id=1, source_target_pairs={{1,0},{2,1},{3,2},{4,3},{5,4},{6,5},{7,6},{9,8},{10,9},{11,10},{12... | collective-permute-start | bytes 786440 | tf_op jit(solution)/shard_map/ppermute | solution.py:22
  29.7 5.6 %collective-permute-done = bf16[1,256,512]{2,0,1:T(2,128)(2,1)} collective-permute-done((bf16[1,256,512]{2,0,1:T(2,128)(2,1)}, bf16[1,256,512]{2,0,1:T(2,128)(2,1)}, u32[]{:S(2)}, u32[]{:S(2)}) %collective-permute-start) | collective-permute-done | bytes 262176 | tf_op jit(solution)/shard_map/ppermute | solution.py:19
  35.3 1.2 collective-permute-done.1
  36.5 6.2 %collective-permute-done.2 = bf16[1,256,512]{2,0,1:T(2,128)(2,1)} collective-permute-done((bf16[1,256,512]{2,0,1:T(2,128)(2,1)S(1)}, bf16[1,256,512]{2,0,1:T(2,128)(2,1)}, u32[]{:S(2)}, u32[]{:S(2)}) %collective-permute-start.2) | collective-permute-done | bytes 262176 | tf_op jit(solution)/shard_map/ppermute | solution.py:19
  42.7 5.4 %collective-permute-done.3 = bf16[1,256,512]{2,0,1:T(2,128)(2,1)} collective-permute-done((bf16[1,256,512]{2,0,1:T(2,128)(2,1)S(1)}, bf16[1,256,512]{2,0,1:T(2,128)(2,1)}, u32[]{:S(2)}, u32[]{:S(2)}) %collective-permute-start.3) | collective-permute-done | bytes 262176 | tf_op jit(solution)/shard_map/ppermute | solution.py:22
  48.0 4.5 %convolution_convert_fusion.1 = bf16[4,256,512]{2,0,1:T(4,128)(2,1)S(1)} fusion(bf16[4,256,512]{2,0,1:T(4,128)(2,1)S(1)} %convolution_convert_fusion.2, bf16[1,256,512]{2,0,1:T(2,128)(2,1)} %collective-permute-done.3, bf16[1,256,512]{2,0,1:T(2,128)(2,1)} %collective-permute-done.2, bf16[1,256,512]{2,0,1:T(2,128)(2,1)} %collective-permute-done.1, ...), kind=kOutput, calls=%fused_computation.36 | convolution fusion | flops 11010064 | bytes 3145760 | tf_op jit(solution)/shard_map/ds,dnj->snj/dot_general | solution.py:68
  52.5 1.4 fusion.27
  55.4 1.7 convolution_bitcast_fusion.2
  57.7 76.7 %all-reduce.2.cloned.1.call-done = f32[1,256,128]{2,1,0:T(8,128)} async-done(((f32[1,256,128]{2,1,0:T(8,128)}), f32[1,256,128]{2,1,0:T(8,128)}) %all-reduce.2.cloned.1.call-update) | async-done | bytes 131088 | tf_op jit(solution)/shard_map/psum | solution.py:138
  135.5 6.2 %all-to-all-start = ((bf16[8,256,256]{1,2,0:T(8,128)(2,1)}), bf16[8,256,256]{1,2,0:T(8,128)(2,1)S(1)}, u32[]{:S(2)}, u32[]{:S(2)}) async-start(bf16[8,256,256]{1,2,0:T(8,128)(2,1)} %stack.7), calls=%async_computation | async-start | bytes 2097152 | tf_op jit(solution)/shard_map/all_to_all | solution.py:11
  142.1 14.6 %reshape_squeeze.6 = bf16[4,512,4,512]{3,2,1,0:T(4,128)(2,1)} reshape(bf16[1,1,2048,2048]{3,2,1,0:T(8,128)(2,1)} %param.18) | data formatting | bytes 16777216 | tf_op jit(solution)/shard_map/reshape;squeeze | solution.py:111
  156.7 7.9 %fusion.9 = f32[256,4,512,1]{2,0,3,1:T(8,128)} fusion(bf16[4,512,4,512]{3,2,1,0:T(4,128)(2,1)} %reshape_squeeze.6, bf16[4,256,512]{2,1,0:T(8,128)(2,1)} %copy-done.3, bf16[4,512]{1,0:T(4,128)(2,1)S(1)} %convert_element_type.89), kind=kOutput, calls=%fused_computation.11 | convolution fusion | flops 2149580800 | bytes 11538432 | tf_op jit(solution)/shard_map/gnj,gjfk->fnk/dot_general | solution.py:113
  165.1 31.2 %all-gather.5.cloned.1.call-done = f32[32,256,128]{2,1,0:T(8,128)} async-done(((f32[1,256,128]{2,1,0:T(8,128)}), f32[32,256,128]{2,1,0:T(8,128)}) %all-gather.5.cloned.1.call-update) | async-done | bytes 4194320 | tf_op jit(solution)/shard_map/all_gather | solution.py:29
  196.3 71.3 %while.14 = (s32[]{:T(128)}, f32[256,128]{0,1:T(8,128)S(1)}, s32[]{:T(128)}, f32[32,128,128]{2,1,0:T(8,128)}, f32[32,256,128]{2,1,0:T(8,128)}, /*index=5*/s32[]{:T(128)}, s32[]{:T(128)}) while((s32[]{:T(128)}, f32[256,128]{0,1:T(8,128)S(1)}, s32[]{:T(128)}, f32[32,128,128]{2,1,0:T(8,128)}, f32[32,256,128]{2,1,0:T(8,128)}, ...), condition=%wide.region_3.4_spmd.clone, body=%wide.region_2.3_spmd.clone.sunk | while | flops 50462724 | bytes 1378403 | solution.py:41
  197.4 1.2 fusion.85
  269.2 2.7 fusion.12
  272.0 3.3 %multiply_convert_fusion = bf16[4,256,512]{2,0,1:T(4,128)(2,1)S(1)} fusion(f32[4,256,512]{2,1,0:T(8,128)S(1)} %fusion.12, f32[4]{0:T(128)S(1)} %bitcast.94, s32[4]{0:T(128)S(1)} %bitcast.90), kind=kOutput, calls=%fused_computation.24 | convolution fusion | flops 26214416 | bytes 3145760 | tf_op jit(solution)/shard_map/ds,snj->dnj/dot_general | solution.py:61
  275.3 1.6 fusion.69
  276.9 2.2 collective-permute-start.4
  279.1 6.4 %collective-permute-start.5 = (bf16[1,256,512]{2,0,1:T(2,128)(2,1)S(1)}, bf16[1,256,512]{2,0,1:T(2,128)(2,1)S(1)}, u32[]{:S(2)}, u32[]{:S(2)}) collective-permute-start(bf16[1,256,512]{2,0,1:T(2,128)(2,1)S(1)} %get-tuple-element.151), channel_id=1, source_target_pairs={{8,0},{16,8},{24,16},{32,24},{40,32},{48,40},{56,48},{64,56},{72,6... | collective-permute-start | bytes 786440 | tf_op jit(solution)/shard_map/ppermute | solution.py:22
  285.5 2.6 collective-permute-start.6
  288.1 3.3 %collective-permute-start.7 = (bf16[1,256,512]{2,0,1:T(2,128)(2,1)S(1)}, bf16[1,256,512]{2,0,1:T(2,128)(2,1)S(1)}, u32[]{:S(2)}, u32[]{:S(2)}) collective-permute-start(bf16[1,256,512]{2,0,1:T(2,128)(2,1)S(1)} %get-tuple-element.149), channel_id=1, source_target_pairs={{1,0},{2,1},{3,2},{4,3},{5,4},{6,5},{7,6},{9,8},{10,9},{11,10},{12... | collective-permute-start | bytes 786440 | tf_op jit(solution)/shard_map/ppermute | solution.py:22
  291.3 6.7 %collective-permute-done.4 = bf16[1,256,512]{2,0,1:T(2,128)(2,1)S(1)} collective-permute-done((bf16[1,256,512]{2,0,1:T(2,128)(2,1)S(1)}, bf16[1,256,512]{2,0,1:T(2,128)(2,1)S(1)}, u32[]{:S(2)}, u32[]{:S(2)}) %collective-permute-start.4) | collective-permute-done | bytes 262176 | tf_op jit(solution)/shard_map/ppermute | solution.py:19
  298.1 4.6 %collective-permute-done.6 = bf16[1,256,512]{2,0,1:T(2,128)(2,1)S(1)} collective-permute-done((bf16[1,256,512]{2,0,1:T(2,128)(2,1)S(1)}, bf16[1,256,512]{2,0,1:T(2,128)(2,1)S(1)}, u32[]{:S(2)}, u32[]{:S(2)}) %collective-permute-start.6) | collective-permute-done | bytes 262176 | tf_op jit(solution)/shard_map/ppermute | solution.py:19
  302.6 7.4 %collective-permute-done.7 = bf16[1,256,512]{2,0,1:T(2,128)(2,1)S(1)} collective-permute-done((bf16[1,256,512]{2,0,1:T(2,128)(2,1)S(1)}, bf16[1,256,512]{2,0,1:T(2,128)(2,1)S(1)}, u32[]{:S(2)}, u32[]{:S(2)}) %collective-permute-start.7) | collective-permute-done | bytes 262176 | tf_op jit(solution)/shard_map/ppermute | solution.py:22
  310.0 2.9 convolution_convert_fusion
  313.0 2.2 fusion.29
  (171 shorter events, 76.3 us)
Async XLA Ops:
  7.4 46.5 %copy-start = (bf16[1,1,2048,256]{3,2,1,0:T(8,128)(2,1)S(1)}, bf16[1,1,2048,256]{3,2,1,0:T(8,128)(2,1)}, u32[]{:S(2)}) copy-start(bf16[1,1,2048,256]{3,2,1,0:T(8,128)(2,1)} %param.19) | copy-start | bytes 3145732
  7.4 127.0 %all-reduce.2.cloned.1.call-start = ((), (), s32[]{:S(2)}) async-start(), calls=%async_computation.2 | async-start | bytes 262144 | tf_op jit(solution)/shard_map/psum | solution.py:138
  7.4 3.5 %copy-start.6 = (s32[1,1,4]{2,1,0:T(1,128)S(1)}, s32[1,1,4]{2,1,0:T(1,128)}, u32[]{:S(2)}) copy-start(s32[1,1,4]{2,1,0:T(1,128)} %param.14) | copy-start | bytes 52
  11.9 36.1 %copy-start.9 = (f32[1,1,4]{2,1,0:T(1,128)S(1)}, f32[1,1,4]{2,1,0:T(1,128)}, u32[]{:S(2)}) copy-start(f32[1,1,4]{2,1,0:T(1,128)} %param.16) | copy-start | bytes 52
  14.3 21.0 %collective-permute-start = (bf16[1,256,512]{2,0,1:T(2,128)(2,1)}, bf16[1,256,512]{2,0,1:T(2,128)(2,1)}, u32[]{:S(2)}, u32[]{:S(2)}) collective-permute-start(bf16[1,256,512]{2,0,1:T(2,128)(2,1)} %get-tuple-element.152), channel_id=1, source_target_pairs={{0,8},{8,16},{16,24},{24,32},{32,40},{40,48},{48,56},{56,64},{64,7... | collective-permute-start | bytes 786440 | tf_op jit(solution)/shard_map/ppermute | solution.py:19
  16.2 20.3 %collective-permute-start.1 = (bf16[1,256,512]{2,0,1:T(2,128)(2,1)}, bf16[1,256,512]{2,0,1:T(2,128)(2,1)}, u32[]{:S(2)}, u32[]{:S(2)}) collective-permute-start(bf16[1,256,512]{2,0,1:T(2,128)(2,1)} %get-tuple-element.155), channel_id=1, source_target_pairs={{8,0},{16,8},{24,16},{32,24},{40,32},{48,40},{56,48},{64,56},{72,6... | collective-permute-start | bytes 786440 | tf_op jit(solution)/shard_map/ppermute | solution.py:22
  23.8 18.8 %collective-permute-start.2 = (bf16[1,256,512]{2,0,1:T(2,128)(2,1)S(1)}, bf16[1,256,512]{2,0,1:T(2,128)(2,1)}, u32[]{:S(2)}, u32[]{:S(2)}) collective-permute-start(bf16[1,256,512]{2,0,1:T(2,128)(2,1)S(1)} %get-tuple-element.154), channel_id=1, source_target_pairs={{0,1},{1,2},{2,3},{3,4},{4,5},{5,6},{6,7},{8,9},{9,10},{10,11},{11... | collective-permute-start | bytes 786440 | tf_op jit(solution)/shard_map/ppermute | solution.py:19
  26.4 21.6 %collective-permute-start.3 = (bf16[1,256,512]{2,0,1:T(2,128)(2,1)S(1)}, bf16[1,256,512]{2,0,1:T(2,128)(2,1)}, u32[]{:S(2)}, u32[]{:S(2)}) collective-permute-start(bf16[1,256,512]{2,0,1:T(2,128)(2,1)S(1)} %get-tuple-element.153), channel_id=1, source_target_pairs={{1,0},{2,1},{3,2},{4,3},{5,4},{6,5},{7,6},{9,8},{10,9},{11,10},{12... | collective-permute-start | bytes 786440 | tf_op jit(solution)/shard_map/ppermute | solution.py:22
  48.0 4.5 %copy-start.5 = (s32[1,1,4,512]{3,2,1,0:T(4,128)S(1)}, s32[1,1,4,512]{3,2,1,0:T(4,128)}, u32[]{:S(2)}) copy-start(s32[1,1,4,512]{3,2,1,0:T(4,128)} %param.15) | copy-start | bytes 24580
  53.9 1.0 copy-start.3
  55.3 86.4 %copy-start.8 = (s32[1,1,256]{2,1,0:T(1,128)S(1)}, s32[1,1,256]{2,1,0:T(1,128)}, u32[]{:S(2)}) copy-start(s32[1,1,256]{2,1,0:T(1,128)} %param.17) | copy-start | bytes 3076
  57.1 108.1 %all-gather.3.cloned.1.call-start = ((), (), s32[]{:S(2)}) async-start(), calls=%async_computation.1 | async-start | bytes 2162688 | tf_op jit(solution)/shard_map/all_gather | solution.py:29
  57.6 138.7 %all-gather.5.cloned.1.call-start = ((), (), s32[]{:S(2)}) async-start(), calls=%async_computation.3 | async-start | bytes 4325376 | tf_op jit(solution)/shard_map/all_gather | solution.py:29
  135.5 29.1 %all-to-all-start = ((bf16[8,256,256]{1,2,0:T(8,128)(2,1)}), bf16[8,256,256]{1,2,0:T(8,128)(2,1)S(1)}, u32[]{:S(2)}, u32[]{:S(2)}) async-start(bf16[8,256,256]{1,2,0:T(8,128)(2,1)} %stack.7), calls=%async_computation | async-start | bytes 2097152 | tf_op jit(solution)/shard_map/all_to_all | solution.py:11
  156.7 8.0 %copy-start.2 = (bf16[1,2048,256]{2,1,0:T(8,128)(2,1)S(1)}, bf16[1,2048,256]{2,1,0:T(8,128)(2,1)}, u32[]{:S(2)}) copy-start(bf16[1,2048,256]{2,1,0:T(8,128)(2,1)} %param.20) | copy-start | bytes 3145732
  196.3 71.3 %copy-start.4 = (bf16[1,128,256]{2,1,0:T(8,128)(2,1)S(1)}, bf16[1,128,256]{2,1,0:T(8,128)(2,1)}, u32[]{:S(2)}) copy-start(bf16[1,128,256]{2,1,0:T(8,128)(2,1)} %param.23) | copy-start | bytes 196612
  267.6 1.6 copy-start.1
  269.2 2.8 copy-start.7
  269.2 2.8 copy-start.10
  276.9 21.2 %collective-permute-start.4 = (bf16[1,256,512]{2,0,1:T(2,128)(2,1)S(1)}, bf16[1,256,512]{2,0,1:T(2,128)(2,1)S(1)}, u32[]{:S(2)}, u32[]{:S(2)}) collective-permute-start(bf16[1,256,512]{2,0,1:T(2,128)(2,1)S(1)} %get-tuple-element.148), channel_id=1, source_target_pairs={{0,8},{8,16},{16,24},{24,32},{32,40},{40,48},{48,56},{56,64},{64,7... | collective-permute-start | bytes 786440 | tf_op jit(solution)/shard_map/ppermute | solution.py:19
  279.1 19.0 %collective-permute-start.5 = (bf16[1,256,512]{2,0,1:T(2,128)(2,1)S(1)}, bf16[1,256,512]{2,0,1:T(2,128)(2,1)S(1)}, u32[]{:S(2)}, u32[]{:S(2)}) collective-permute-start(bf16[1,256,512]{2,0,1:T(2,128)(2,1)S(1)} %get-tuple-element.151), channel_id=1, source_target_pairs={{8,0},{16,8},{24,16},{32,24},{40,32},{48,40},{56,48},{64,56},{72,6... | collective-permute-start | bytes 786440 | tf_op jit(solution)/shard_map/ppermute | solution.py:22
  285.5 17.1 %collective-permute-start.6 = (bf16[1,256,512]{2,0,1:T(2,128)(2,1)S(1)}, bf16[1,256,512]{2,0,1:T(2,128)(2,1)S(1)}, u32[]{:S(2)}, u32[]{:S(2)}) collective-permute-start(bf16[1,256,512]{2,0,1:T(2,128)(2,1)S(1)} %get-tuple-element.150), channel_id=1, source_target_pairs={{0,1},{1,2},{2,3},{3,4},{4,5},{5,6},{6,7},{8,9},{9,10},{10,11},{11... | collective-permute-start | bytes 786440 | tf_op jit(solution)/shard_map/ppermute | solution.py:19
  288.1 22.0 %collective-permute-start.7 = (bf16[1,256,512]{2,0,1:T(2,128)(2,1)S(1)}, bf16[1,256,512]{2,0,1:T(2,128)(2,1)S(1)}, u32[]{:S(2)}, u32[]{:S(2)}) collective-permute-start(bf16[1,256,512]{2,0,1:T(2,128)(2,1)S(1)} %get-tuple-element.149), channel_id=1, source_target_pairs={{1,0},{2,1},{3,2},{4,3},{5,4},{6,5},{7,6},{9,8},{10,9},{11,10},{12... | collective-permute-start | bytes 786440 | tf_op jit(solution)/shard_map/ppermute | solution.py:22
Sparse Core Ops, SparseCore 0:
  57.2 77.1 all-reduce.1
Sparse Core Ops, SparseCore 1:
  60.1 54.1 all-gather.2
  134.5 61.8 all-gather.4
